TPU v7x, 256 devices: a whole 4x4x8 slice. The times are simulated.
256 devices in a mesh: seq: 16 (over y, x_lo, core), fsdp: 16 (over z, x_hi).
Axes of the slice: x: 4 (x_hi: 2, x_lo: 2; x = x_hi * 2 + x_lo), y: 4, z: 8, core: 2. Of those that a mesh axis runs over, the one named last changes fastest.
Arguments:
- clean_states: bfloat16 [16, 4096, 4096], P('fsdp', 'seq'), may hold values from -6 to 6
- noise_mask: int32 [16, 4096], P('fsdp', 'seq'), may hold values from 0 to 1, as said below
- mask_embed: bfloat16 [4096], replicated, may hold values from -6 to 6
- queries: bfloat16 [16, 4096, 2048], P('fsdp', 'seq'), may hold values from -96 to 96
- w_key: bfloat16 [4096, 512], P('fsdp'), may hold values from -0.09375 to 0.09375
- w_value: bfloat16 [4096, 512], P('fsdp'), may hold values from -0.09375 to 0.09375
Outputs:
- noisy_attention: bfloat16 [16, 4096, 2048], P('fsdp', 'seq')
Inputs may be any that keep to these rules, and one draw needn't show every extreme that they name: `noise_mask`: each block of 256 positions has its own masking rate; 1 marks a masked position.
All inputs are finite; a program needn't handle non-finite values.
Results may differ from a plain program's by a relative error of at most 0.011.
Values may be sent and summed in bfloat16 or wider, within the bound.
A program may use at most 64 MiB of HBM per device.

v0:
```python
import jax
import jax.numpy as jnp
from jax import lax
from jax.sharding import PartitionSpec as P

HEADS = 16
HEAD_DIM = 128
BLOCK = 256


ROPE_BASE = 500000.0


def rotate(key_rows, positions):
    half_dim = key_rows.shape[-1] // 2
    frequency = ROPE_BASE ** (-(jnp.arange(half_dim, dtype=jnp.float32) * 2.0 / key_rows.shape[-1]))
    angles = positions[:, None] * frequency[None, :]
    cosine = jnp.cos(angles)[:, None, :]
    sine_part = jnp.sin(angles)[:, None, :]
    first_half = key_rows[..., :half_dim]
    second_half = key_rows[..., half_dim:]
    return jnp.concatenate(
        [
            first_half * cosine - second_half * sine_part,
            second_half * cosine + first_half * sine_part,
        ],
        -1,
    )


def shards(clean_states, noise_mask, mask_embed, queries, w_key, w_value):
    states = clean_states[0]
    noise_marks = noise_mask[0]
    length_dev = states.shape[0]
    kv_width = w_key.shape[1]
    kv_count = kv_width // HEAD_DIM
    groups = HEADS // kv_count
    score_scale = HEAD_DIM ** (-0.5)
    query_rows = queries[0].reshape(length_dev, kv_count, groups, HEAD_DIM)
    source_rows = jnp.concatenate([states, mask_embed[None, :]], 0)
    pieces = (
        lax.all_gather(w_key, "fsdp", axis=0, tiled=True),
        lax.all_gather(w_value, "fsdp", axis=0, tiled=True),
    )
    key_all = jnp.dot(source_rows, pieces[0], preferred_element_type=jnp.float32)
    value_all = jnp.dot(source_rows, pieces[1], preferred_element_type=jnp.float32)
    masked_rows = noise_marks[:, None] == 1
    clean_key_sums = key_all[:length_dev]
    clean_value_sums = value_all[:length_dev]
    noisy_key_sums = jnp.where(masked_rows, key_all[length_dev:], clean_key_sums)
    noisy_value_sums = jnp.where(masked_rows, value_all[length_dev:], clean_value_sums)
    key_sums = jnp.concatenate([clean_key_sums, noisy_key_sums], 0)
    value_sums = jnp.concatenate([clean_value_sums, noisy_value_sums], 0)
    first_row = lax.axis_index("seq") * length_dev
    positions = first_row + jnp.arange(length_dev, dtype=jnp.int32)
    both_positions = jnp.concatenate([positions, positions]).astype(jnp.float32)
    key_rows = (
        rotate(key_sums.reshape(2 * length_dev, kv_count, HEAD_DIM), both_positions)
        .astype(jnp.bfloat16)
        .reshape(2 * length_dev, kv_width)
    )
    value_rows = value_sums.astype(jnp.bfloat16)
    clean_keys = key_rows[:length_dev]
    clean_values = value_rows[:length_dev]
    noisy_keys = key_rows[length_dev:]
    noisy_values = value_rows[length_dev:]
    query_block = positions // BLOCK

    def absorb(running, key_part, value_part, allowed):
        row_max, row_sum, mixture = running
        key_count = key_part.shape[0]
        scores = (
            jnp.einsum(
                "qkgd,tkd->qkgt",
                query_rows,
                key_part.reshape(key_count, kv_count, HEAD_DIM),
                preferred_element_type=jnp.float32,
            )
            * score_scale
        )
        mask_wide = allowed[:, None, None, :]
        scores = jnp.where(mask_wide, scores, -1e30)
        new_max = jnp.maximum(row_max, jnp.max(scores, -1))
        weights = jnp.where(mask_wide, jnp.exp(scores - new_max[..., None]), 0.0)
        rescale = jnp.exp(row_max - new_max)
        row_sum = row_sum * rescale + jnp.sum(weights, -1)
        mixture = mixture * rescale[..., None] + jnp.einsum(
            "qkgt,tkd->qkgd",
            weights.astype(jnp.bfloat16),
            value_part.reshape(key_count, kv_count, HEAD_DIM),
            preferred_element_type=jnp.float32,
        )
        return (new_max, row_sum, mixture)

    def sweep(running, key_stack, value_stack, start_row, same_copy):
        rounds = key_stack.shape[0] // BLOCK

        def sub_step(number, running):
            offset = number * BLOCK
            key_part = lax.dynamic_slice_in_dim(key_stack, offset, BLOCK, 0)
            value_part = lax.dynamic_slice_in_dim(value_stack, offset, BLOCK, 0)
            key_block = (start_row + offset) // BLOCK
            if same_copy:
                allowed = query_block[:, None] == key_block
            else:
                allowed = (query_block[:, None] > key_block) & (key_block >= 0)
            allowed = jnp.broadcast_to(allowed, (length_dev, BLOCK))
            return absorb(running, key_part, value_part, allowed)

        return lax.fori_loop(0, rounds, sub_step, running)

    running = (
        jnp.full((length_dev, kv_count, groups), -1e30, jnp.float32),
        jnp.zeros((length_dev, kv_count, groups), jnp.float32),
        jnp.zeros((length_dev, kv_count, groups, HEAD_DIM), jnp.float32),
    )
    running = sweep(running, noisy_keys, noisy_values, first_row, True)
    pieces = (
        lax.all_gather(clean_keys, "seq", axis=0, tiled=True),
        lax.all_gather(clean_values, "seq", axis=0, tiled=True),
    )
    running = sweep(running, pieces[0], pieces[1], jnp.int32(0), False)
    row_max, row_sum, mixture = running
    output = (
        (mixture / row_sum[..., None])
        .astype(jnp.bfloat16)
        .reshape(length_dev, kv_count * groups * HEAD_DIM)
    )
    return output[None]


def solution(mesh):
    placed = (
        P("fsdp", "seq", None),
        P("fsdp", "seq"),
        P(),
        P("fsdp", "seq", None),
        P("fsdp", None),
        P("fsdp", None),
    )
    return jax.shard_map(
        shards, mesh=mesh, in_specs=placed, out_specs=P("fsdp", "seq", None), check_vma=False
    )
```

profile of v0, /device:TPU:3, one launch (start us, length us, event | category | flops | bytes accessed | tf_op | source)
XLA Modules:
  0.0 418.7 jit_solution(12876547095858596038)
XLA Ops:
  9.5 99.3 %all-gather.7.cloned.1.call-done = bf16[4096,512]{1,0:T(8,128)(2,1)} async-done(((bf16[256,512]{1,0:T(8,128)(2,1)}), bf16[4096,512]{1,0:T(8,128)(2,1)}) %all-gather.7.cloned.1.call-update) | async-done | bytes 4194320 | tf_op jit(solution)/shard_map/all_gather | solution.py:43
  108.8 4.2 %fusion.33 = f32[257,512]{1,0:T(8,128)S(1)} fusion(bf16[4096,512]{1,0:T(8,128)(2,1)} %all-gather.7.cloned.1.call-done, bf16[1,4096]{1,0:T(2,128)(2,1)S(1)} %broadcast_in_dim.141, bf16[256,4096]{1,0:T(8,128)(2,1)} %bitcast.118), kind=kOutput, calls=%fused_computation.45 | convolution fusion | flops 1082146816 | bytes 6825984 | tf_op jit(solution)/shard_map/dot_general | solution.py:46
  113.9 1.0 multiply_cosine_fusion
  114.9 93.1 %all-gather.5.cloned.1.call-done = bf16[4096,512]{1,0:T(8,128)(2,1)} async-done(((bf16[256,512]{1,0:T(8,128)(2,1)}), bf16[4096,512]{1,0:T(8,128)(2,1)}) %all-gather.5.cloned.1.call-update) | async-done | bytes 4194320 | tf_op jit(solution)/shard_map/all_gather | solution.py:42
  208.0 3.5 fusion.34
  214.0 1.5 copy.18
  217.9 1.0 fusion.22
  219.0 2.5 bitcast_add_fusion.1
  221.5 29.1 %all-gather.11.cloned.1.call-done = bf16[4096,512]{1,0:T(8,128)(2,1)} async-done(((bf16[256,512]{1,0:T(8,128)(2,1)}), bf16[4096,512]{1,0:T(8,128)(2,1)}) %all-gather.11.cloned.1.call-update) | async-done | bytes 4194320 | tf_op jit(solution)/shard_map/all_gather | solution.py:120
  250.6 49.7 %all-gather.9.cloned.1.call-done = bf16[4096,512]{0,1:T(8,128)(2,1)} async-done(((bf16[256,512]{0,1:T(8,128)(2,1)}), bf16[4096,512]{0,1:T(8,128)(2,1)}) %all-gather.9.cloned.1.call-update) | async-done | bytes 4194320 | tf_op jit(solution)/shard_map/all_gather | solution.py:119
  300.2 108.7 %while.13 = (s32[]{:T(128)}, f32[256,4,4]{0,2,1:T(4,128)S(1)}, f32[256,4,4]{0,2,1:T(4,128)S(1)}, f32[256,4,4,128]{0,3,2,1:T(8,128)}, bf16[4096,512]{0,1:T(8,128)...) while((s32[]{:T(128)}, f32[256,4,4]{0,2,1:T(4,128)S(1)}, ...), condition=%wide.region_5.6_spmd.clone, body=%wide.region_2.5_spmd.clone.sunk | while | flops 551563776 | bytes 36963736 | solution.py:110
  301.3 1.0 constant_dynamic-slice_fusion.4
  303.2 1.0 fusion.66
  304.2 1.4 bitcast_add_fusion.3
  305.6 1.4 copy-done.1
  308.1 1.0 constant_dynamic-slice_fusion.4
  310.0 1.0 fusion.66
  311.0 1.4 bitcast_add_fusion.3
  312.4 1.4 copy-done.1
  316.8 1.0 fusion.66
  317.8 1.4 bitcast_add_fusion.3
  319.2 1.4 copy-done.1
  323.6 1.0 fusion.66
  324.6 1.4 bitcast_add_fusion.3
  326.0 1.4 copy-done.1
  330.3 1.0 fusion.66
  331.4 1.4 bitcast_add_fusion.3
  332.8 1.4 copy-done.1
  337.1 1.0 fusion.66
  338.2 1.4 bitcast_add_fusion.3
  339.6 1.4 copy-done.1
  343.9 1.0 fusion.66
  345.0 1.4 bitcast_add_fusion.3
  346.4 1.4 copy-done.1
  350.7 1.0 fusion.66
  351.8 1.4 bitcast_add_fusion.3
  353.2 1.4 copy-done.1
  357.5 1.0 fusion.66
  358.6 1.4 bitcast_add_fusion.3
  360.0 1.4 copy-done.1
  364.3 1.0 fusion.66
  365.4 1.4 bitcast_add_fusion.3
  366.8 1.4 copy-done.1
  371.1 1.0 fusion.66
  372.2 1.4 bitcast_add_fusion.3
  373.6 1.4 copy-done.1
  376.1 1.0 constant_dynamic-slice_fusion.4
  377.9 1.0 fusion.66
  379.0 1.4 bitcast_add_fusion.3
  380.4 1.4 copy-done.1
  384.7 1.0 fusion.66
  385.7 1.4 bitcast_add_fusion.3
  387.2 1.4 copy-done.1
  391.5 1.0 fusion.66
  392.5 1.4 bitcast_add_fusion.3
  394.0 1.4 copy-done.1
  398.3 1.0 fusion.66
  399.3 1.4 bitcast_add_fusion.3
  400.8 1.4 copy-done.1
  405.1 1.0 fusion.66
  406.1 1.4 bitcast_add_fusion.3
  407.5 1.4 copy-done.1
  408.9 1.8 divide_convert_fusion
  410.7 1.4 copy.34
  (206 shorter events, 53.0 us)
Async XLA Ops:
  6.5 102.3 %all-gather.7.cloned.1.call-start = ((), (), s32[]{:S(2)}) async-start(), calls=%async_computation.1 | async-start | bytes 4456448 | tf_op jit(solution)/shard_map/all_gather | solution.py:43
  7.3 200.7 %all-gather.5.cloned.1.call-start = ((), (), s32[]{:S(2)}) async-start(), calls=%async_computation | async-start | bytes 4456448 | tf_op jit(solution)/shard_map/all_gather | solution.py:42
  8.0 242.5 %all-gather.11.cloned.1.call-start = ((), (), s32[]{:S(2)}) async-start(), calls=%async_computation.3 | async-start | bytes 4456448 | tf_op jit(solution)/shard_map/all_gather | solution.py:120
  108.8 99.2 %copy-start.3 = (bf16[1,256,4096]{2,1,0:T(8,128)(2,1)S(1)}, bf16[1,256,4096]{2,1,0:T(8,128)(2,1)}, u32[]{:S(2)}) copy-start(bf16[1,256,4096]{2,1,0:T(8,128)(2,1)} %param.8) | copy-start | bytes 6291460
  113.8 186.4 %all-gather.9.cloned.1.call-start = ((), (), s32[]{:S(2)}) async-start(), calls=%async_computation.2 | async-start | bytes 4456448 | tf_op jit(solution)/shard_map/all_gather | solution.py:119
  217.0 1.9 copy-start.2
  302.3 1.9 copy-start
  305.6 1.4 copy-start.1
  309.1 1.9 copy-start
  312.4 1.4 copy-start.1
  315.9 1.9 copy-start
  319.2 1.4 copy-start.1
  322.7 1.9 copy-start
  326.0 1.4 copy-start.1
  329.5 1.9 copy-start
  332.8 1.4 copy-start.1
  336.3 1.9 copy-start
  339.6 1.4 copy-start.1
  343.1 1.9 copy-start
  346.4 1.4 copy-start.1
  349.9 1.9 copy-start
  353.2 1.4 copy-start.1
  356.7 1.9 copy-start
  360.0 1.4 copy-start.1
  363.5 1.9 copy-start
  366.8 1.4 copy-start.1
  370.2 1.9 copy-start
  373.6 1.4 copy-start.1
  377.0 1.9 copy-start
  380.4 1.4 copy-start.1
  383.8 1.9 copy-start
  387.1 1.4 copy-start.1
  390.6 1.9 copy-start
  393.9 1.4 copy-start.1
  397.4 1.9 copy-start
  400.7 1.4 copy-start.1
  404.2 1.9 copy-start
  407.5 1.4 copy-start.1
Sparse Core Ops, SparseCore 0:
  9.9 98.8 all-gather.6
  111.4 96.5 all-gather.4
  209.8 40.6 all-gather.10
  252.2 47.9 all-gather.8
where the time goes:
time: 422 us; the launch traced here: 419 us
  waiting for transfers between devices  273 us (65%)
  local copies, waits for them, and re-layouts  62 us (15%)
  matrix products  46.7 us (11%)
  other arithmetic  22.8 us (5%)
  between operations  13.3 us (3%)
    all_gather x1, waiting for transfers between devices, shards(): lax.all_gather(w_value, 'fsdp', axis=0, tiled=True)  99.3 us
    all_gather x1, waiting for transfers between devices, shards(): lax.all_gather(w_key, 'fsdp', axis=0, tiled=True)  93.1 us
    all_gather x1, waiting for transfers between devices, shards(): lax.all_gather(clean_keys, 'seq', axis=0, tiled=True)  49.7 us
    all_gather x1, waiting for transfers between devices, shards(): lax.all_gather(clean_values, 'seq', axis=0, tiled=True)  29.1 us
    dot_general x17, matrix products, absorb(): jnp.einsum('qkgt,tkd->qkgd', weights.astype(jnp.bfloat16), value_part.res...  24.7 us
    while x80, local copies, waits for them, and re-layouts  21.8 us
    dynamic_slice x32, local copies, waits for them, and re-layouts, sub_step(): value_part = lax.dynamic_slice_in_dim(value_stack, offset, BLOCK, 0)  17.7 us
    reduce_sum x17, other arithmetic, absorb(): row_sum = row_sum * rescale + jnp.sum(weights, -1)  17.4 us
  transfers between devices with their start and end apart: 4, of which 4 were waited for; matrix products, arithmetic and copies ran while one was open for 5% of the time, Pallas kernels for 0%

commit v1 on v0

v1 whole, which is shorter than its diff:
```python
import jax
import jax.numpy as jnp
import numpy as np
from jax import lax
from jax.experimental import pallas as pl
from jax.experimental.pallas import tpu as pltpu
from jax.sharding import PartitionSpec as P

MESH = pl.DeviceIdType.MESH
BF16 = jnp.bfloat16
F32 = jnp.float32
HEAD_DIM = 128
BLOCK = 256
ROPE_BASE = 500000.0
SCORE_SCALE = float(HEAD_DIM**-0.5 * np.log2(np.e))
NT = (((1,), (1,)), ((), ()))

ROUTE = {
    (0, 1, 0): "y+", (0, 1, 1): "y-", (1, 1, 0): "xl", (1, 1, 1): "y+",
    (0, 2, 0): "y-", (0, 2, 1): "xl", (1, 2, 0): "xh", (1, 2, 1): "xh",
    (0, 3, 0): "y+", (0, 3, 1): "y-", (1, 3, 0): "xl", (1, 3, 1): "y+",
    (0, 4, 0): "y-", (0, 4, 1): "xl", (1, 4, 0): "y-", (1, 4, 1): "xl",
}
OPPOSITE = {"y+": "y-", "y-": "y+", "xl": "xl", "xh": "xh"}
KV_ORDER = ((0, 1), (1, 0), (3, 0), (1, 1), (3, 1), (2, 0), (2, 1))

EV_X, EV_XH, EV_Z, EV_P = 0, 1, 3, 19
EV_Q, EV_M, EV_K, EV_V, EV_O = 35, 38, 41, 49, 57
EV_COUNT = 60


def event(ring, distance, other):
    return (ring * 4 + distance - 1) * 2 + other


def kernel(
    states, marks, mask_row, queries, w_key, w_value, cosine, sine, far_cosine, far_sine, out,
    x_buf, w_buf, sums, k_own, v_own, k_all, v_all, q_buf, m_buf, o_buf,
    tables, row_max, mix, send_sem, recv_sem, local_sem,
):
    seq = lax.axis_index("seq")
    fsdp = lax.axis_index("fsdp")
    core = seq % 2
    chip = seq // 2
    xl = chip % 2
    y = chip // 2
    z = fsdp // 2
    xh = fsdp % 2
    role = y % 2
    side = (y + xl) % 2
    mate = (3 - y) * 2 + xl

    def at(yy, xx, cc):
        return ((yy % 4 * 2 + xx) * 2 + cc, fsdp)

    near = {
        "y+": at(y + 1, xl, core),
        "y-": at(y + 3, xl, core),
        "xl": at(y, 1 - xl, core),
        "xh": (at(y, 1 - xl, core)[0], z * 2 + 1 - xh),
        "z+": (seq, (z + 1) % 8 * 2 + xh),
        "z-": (seq, (z + 7) % 8 * 2 + xh),
        "core": at(y, xl, 1 - core),
        "mate": at(3 - y, xl, core),
        "mate2": at(3 - y, xl, 1 - core),
    }

    def remote(src, dst, number, device):
        return pltpu.make_async_remote_copy(
            src, dst, send_sem.at[number], recv_sem.at[number],
            device_id=device, device_id_type=MESH,
        )

    locals_ = []

    def local(src, dst, number):
        copy = pltpu.make_async_copy(src, dst, local_sem.at[number])
        copy.start()
        return copy

    wide = pl.ds(pl.multiple_of(core * 256, 256), 256)
    own = fsdp * 2
    load_w = []
    for half in range(2):
        rows = pl.ds(half * 128, 128)
        load_w.append(local(w_key.at[rows, wide], w_buf.at[own + half, :, pl.ds(0, 256)], half * 2))
        load_w.append(local(w_value.at[rows, wide], w_buf.at[own + half, :, pl.ds(256, 256)], half * 2 + 1))
    my_rows = pl.ds(pl.multiple_of(core * 256, 256), 256)
    load_x = local(states, x_buf.at[my_rows, :], 4)
    head = 2 * core + role
    q_cols = pl.ds(pl.multiple_of(head * 512, 512), 512)
    load_q = local(queries.at[:, q_cols], q_buf.at[core], 5)
    load_t = []
    for number, table in enumerate((cosine, sine)):
        load_t.append(local(table, tables.at[number], 6 + number))

    peers = [at(y + dy, xl if dx == 0 else 1 - xl, core) for dy, dx in KV_ORDER]
    peers += [near["core"], near["mate2"], near["xh"], near["z+"], near["z-"]]
    barrier = pltpu.get_barrier_semaphore()
    for peer in peers:
        pl.semaphore_signal(barrier, inc=1, device_id=peer, device_id_type=MESH)
    pl.semaphore_wait(barrier, len(peers))

    sends = []

    def send(src, dst, number, device):
        copy = remote(src, dst, number, device)
        copy.start()
        sends.append(copy)

    for copy in load_w:
        copy.wait()
    other = (z * 2 + 1 - xh) * 2

    def piece(zz, flip, half):
        aa = 1 - xh if flip else xh
        return (zz % 8 * 2 + aa) * 2 + half

    def part(distance, ring):
        if distance < 4:
            return pl.ds(0, 128)
        return pl.ds(ring * 64, 64)

    def ring_send(ring, distance, flip):
        source = z - (distance - 1) if ring == 0 else z + (distance - 1)
        ref = w_buf.at[piece(source + 8, flip, side), part(distance, ring), :]
        send(ref, ref, EV_Z + event(ring, distance, flip), near["z+" if ring == 0 else "z-"])

    send(w_buf.at[own + 1 - side], w_buf.at[own + 1 - side], EV_XH, near["xh"])
    for ring in range(2):
        ring_send(ring, 1, 0)
    send(w_buf.at[own + side], w_buf.at[own + side], EV_XH + 1, near["xh"])
    send(states, x_buf.at[my_rows, :], EV_X, near["core"])

    x_buf[pl.ds(512, 16), :] = jnp.broadcast_to(mask_row[...], (16, mask_row.shape[1]))
    flags = jnp.broadcast_to(marks[...].astype(F32), (128, 256))
    m_buf[core] = jnp.transpose(flags).astype(BF16)
    v_all[:, pl.ds(128, 128)] = jnp.ones((v_all.shape[0], 128), BF16)
    row_max[...] = jnp.full(row_max.shape, -1e30, F32)
    mix[...] = jnp.zeros(mix.shape, F32)

    for copy in load_t:
        copy.wait()
    near_c, near_s = tables[0], tables[1]
    for pair, where in ((1, mate), (0, chip)):
        far_c, far_s = far_cosine[pl.ds(where, 1), :], far_sine[pl.ds(where, 1), :]
        tables[pair * 2] = near_c * far_c - near_s * far_s
        tables[pair * 2 + 1] = near_s * far_c + near_c * far_s

    landing = w_buf.at[other + side]
    remote(landing, landing, EV_XH, near["xh"]).wait_recv()
    for ring in range(2):
        ring_send(ring, 1, 1)

    def q_at(kv_head):
        return queries.at[:, pl.ds(pl.multiple_of(kv_head * 512, 512), 512)]

    send(q_at(2 * (1 - core) + role), q_buf.at[core], EV_Q, near["core"])
    send(m_buf.at[core], m_buf.at[core], EV_M, near["core"])
    send(m_buf.at[core], m_buf.at[2 + core], EV_M + 1, near["mate"])
    send(m_buf.at[core], m_buf.at[2 + core], EV_M + 2, near["mate2"])

    load_x.wait()
    theirs = x_buf.at[pl.ds(pl.multiple_of((1 - core) * 256, 256), 256), :]
    remote(theirs, theirs, EV_X, near["core"]).wait_recv()
    landing = w_buf.at[other + 1 - side]
    remote(landing, landing, EV_XH + 1, near["xh"]).wait_recv()

    def project(zz, first=False):
        zz = zz % 8
        weights = w_buf[pl.ds(zz * 4, 4)].reshape(512, 512)
        rows = x_buf[:, pl.ds(pl.multiple_of(zz * 512, 512), 512)]
        term = jnp.dot(rows, weights, preferred_element_type=F32)
        if first:
            sums[...] = term
        else:
            sums[...] += term

    project(z, True)

    def plane_wait(distance):
        for ring in range(2):
            source = z - distance if ring == 0 else z + distance
            for flip in range(2):
                way = ROUTE[ring, distance, flip]
                ref = w_buf.at[piece(source + 8, flip, 1 - side), part(distance, ring), :]
                remote(ref, ref, EV_P + event(ring, distance, flip), near[OPPOSITE[way]]).wait_recv()

    for distance in range(1, 5):
        for flip in range(2):
            for ring in range(2):
                source = z - distance if ring == 0 else z + distance
                ref = w_buf.at[piece(source + 8, flip, side), part(distance, ring), :]
                number = event(ring, distance, flip)
                remote(ref, ref, EV_Z + number, near["z-" if ring == 0 else "z+"]).wait_recv()
                if distance < 4:
                    ring_send(ring, distance + 1, flip)
                way = ROUTE[ring, distance, flip]
                if way != "xh":
                    send(ref, ref, EV_P + number, near[way])
                elif flip == 1:
                    for mine in range(2):
                        ref = w_buf.at[piece(source + 8, 1 - mine, side), part(distance, ring), :]
                        send(ref, ref, EV_P + event(ring, distance, mine), near["xh"])
        if distance == 1:
            send(q_at(2 * core + 1 - role), q_buf.at[2 + core], EV_Q + 1, near["mate"])
            send(q_at(2 * (1 - core) + 1 - role), q_buf.at[2 + core], EV_Q + 2, near["mate2"])
        else:
            plane_wait(distance - 1)
            project(z + 8 - distance + 1)
            project(z + distance - 1)
    plane_wait(4)
    project(z + 4)

    def rotate(rows, pair, first, count):
        turned = pltpu.roll(rows, 64, 1)
        span = pl.ds(first, count)
        return rows * tables[pair * 2, span, :] + turned * tables[pair * 2 + 1, span, :]

    for kind in range(2):
        keys = sums[pl.ds(0, 512), pl.ds(kind * 128, 128)]
        k_own[kind] = rotate(keys, 0, 0, 512).astype(BF16)
        v_own[kind] = sums[pl.ds(0, 512), pl.ds(256 + kind * 128, 128)].astype(BF16)

    def kv_rows(where):
        return pl.ds(pl.multiple_of(where * 512, 512), 512)

    def k_at(where):
        return k_all.at[kv_rows(where), :]

    def v_at(where):
        return v_all.at[kv_rows(where), pl.ds(0, 128)]

    for dy, dx in KV_ORDER:
        device = at(y + dy, xl if dx == 0 else 1 - xl, core)
        kind = (role + dy) % 2
        send(k_own.at[kind], k_at(chip), EV_K + dy * 2 + dx, device)
        send(v_own.at[kind], v_at(chip), EV_V + dy * 2 + dx, device)
    k_all[kv_rows(chip), :] = k_own[role]
    v_all[kv_rows(chip), pl.ds(0, 128)] = v_own[role]

    load_q.wait()
    for number, slot, device in (
        (EV_Q, 1 - core, near["core"]),
        (EV_Q + 1, 2 + core, near["mate"]),
        (EV_Q + 2, 3 - core, near["mate2"]),
    ):
        remote(q_buf.at[slot], q_buf.at[slot], number, device).wait_recv()
        mark = number - EV_Q + EV_M
        remote(m_buf.at[slot], m_buf.at[slot], mark, device).wait_recv()

    mask_key = sums[pl.ds(512, 16), pl.ds(pl.multiple_of(role * 128, 128), 128)]
    mask_value = sums[pl.ds(512, 16), pl.ds(pl.multiple_of(256 + role * 128, 128), 128)]
    mask_key = jnp.broadcast_to(mask_key[0:1, :], (256, 128))
    mask_value = jnp.broadcast_to(mask_value[0:1, :], (256, 128)).astype(BF16).astype(F32)

    def build(pair, quad):
        for i in range(2):
            slot = pair * 2 + i
            mine = 2 * xl + i
            base = 4096 + slot * 1024
            block = pl.multiple_of((quad * 4 + mine) * 256, 256)
            masked = m_buf[slot].astype(F32) > 0.5
            noisy_k = jnp.where(
                masked,
                rotate(mask_key, pair, i * 256, 256),
                k_all[pl.ds(block, 256), :].astype(F32),
            ).astype(BF16)
            noisy_v = jnp.where(
                masked, mask_value, v_all[pl.ds(block, 256), pl.ds(0, 128)].astype(F32)
            ).astype(BF16)
            for j in range(4):
                rows = pl.ds(base + j * 256, 256)
                start = pl.multiple_of((quad * 4 + j) * 256, 256)

                @pl.when(j < mine)
                def _():
                    k_all[rows, :] = k_all[pl.ds(start, 256), :]
                    v_all[rows, pl.ds(0, 128)] = v_all[pl.ds(start, 256), pl.ds(0, 128)]

                @pl.when(j >= mine)
                def _():
                    k_all[rows, :] = noisy_k

                @pl.when(j == mine)
                def _():
                    v_all[rows, pl.ds(0, 128)] = noisy_v

                @pl.when(j > mine)
                def _():
                    v_all[rows, :] = jnp.zeros((256, 256), BF16)

    def absorb(slot, start):
        span = pl.ds(pl.multiple_of(start, 1024), 1024)
        for g in range(4):
            query = q_buf[slot, :, pl.ds(g * 128, 128)]
            scores = lax.dot_general(query, k_all[span, :], NT, preferred_element_type=F32)
            before = row_max[slot * 4 + g]
            after = jnp.maximum(before, jnp.max(scores, 1, keepdims=True))
            shrink = jnp.exp2((before - after) * SCORE_SCALE)
            probs = jnp.exp2((scores - after[:, :1]) * SCORE_SCALE).astype(BF16)
            term = jnp.dot(probs, v_all[span, :], preferred_element_type=F32)
            for part_ in range(2):
                lanes = pl.ds(part_ * 128, 128)
                mix[slot * 4 + g, :, lanes] = (
                    mix[slot * 4 + g, :, lanes] * shrink + term[:, part_ * 128 : part_ * 128 + 128]
                )
            row_max[slot * 4 + g] = after

    def finish(slot):
        for g in range(4):
            total = mix[slot * 4 + g]
            o_buf[slot, :, pl.ds(g * 128, 128)] = (total[:, :128] / total[:, 128:]).astype(BF16)

    def wait_kv(source, dy, dx):
        where = source * 2 + (xl if dx == 0 else 1 - xl)
        device = at(source, xl if dx == 0 else 1 - xl, core)
        remote(k_at(where), k_at(where), EV_K + dy * 2 + dx, device).wait_recv()
        remote(v_at(where), v_at(where), EV_V + dy * 2 + dx, device).wait_recv()

    def step(number, carry):
        dy = jnp.where(number == 2, 3, number)
        quad = (y + 4 - dy) % 4

        @pl.when(number > 0)
        def _():
            wait_kv(quad, dy, 0)

        wait_kv(quad, dy, 1)

        @pl.when(number == 0)
        def _():
            build(0, quad)

        @pl.when(quad == 3 - y)
        def _():
            build(1, quad)

        def item(kind, carry):
            pair = jnp.where((kind == 1) | (kind == 2), 1, 0)
            level = jnp.where(pair == 1, 3 - y, y)
            active = jnp.where(kind < 2, quad == level, quad < level)

            @pl.when(active)
            def _():
                def one(i, carry):
                    slot = pair * 2 + i
                    absorb(slot, jnp.where(kind < 2, 4096 + slot * 1024, quad * 1024))
                    return carry

                lax.fori_loop(0, 2, one, 0)

            return carry

        lax.fori_loop(0, 4, item, 0)
        return carry

    lax.fori_loop(0, 3, step, 0)

    last = (y + 2) % 4
    wait_kv(last, 2, 0)
    wait_kv(last, 2, 1)
    out_cols = pl.ds(pl.multiple_of(head * 512, 512), 512)

    def final(i, carry):
        slot = (i + 2) % 4

        @pl.when(last < jnp.where(slot >= 2, 3 - y, y))
        def _():
            absorb(slot, last * 1024)

        finish(slot)

        @pl.when(slot >= 2)
        def _():
            remote(
                o_buf.at[slot], out.at[:, out_cols], EV_O + (slot - core + 2) % 2,
                at(3 - y, xl, slot % 2),
            ).start()

        return carry

    lax.fori_loop(0, 4, final, 0)
    send(o_buf.at[1 - core], out.at[:, out_cols], EV_O + 2, near["core"])
    store = local(o_buf.at[core], out.at[:, out_cols], 5)
    store.wait()

    def o_at(kv_head):
        return out.at[:, pl.ds(pl.multiple_of(kv_head * 512, 512), 512)]

    for number, kv_head, device in (
        (EV_O, 2 * core + 1 - role, near["mate"]),
        (EV_O + 1, 2 * (1 - core) + 1 - role, near["mate2"]),
        (EV_O + 2, 2 * (1 - core) + role, near["core"]),
    ):
        remote(o_at(kv_head), o_at(kv_head), number, device).wait_recv()
    for number in range(2):
        slot = 2 + (core + number) % 2
        remote(o_buf.at[slot], out.at[:, out_cols], EV_O + number, at(3 - y, xl, slot % 2)).wait_send()
    for copy in sends:
        copy.wait_send()


def tables_of(positions):
    half = HEAD_DIM // 2
    steps = np.arange(half, dtype=np.float32) * np.float32(2.0) / np.float32(HEAD_DIM)
    frequency = (np.float32(ROPE_BASE) ** (-steps)).astype(np.float64)
    angles = positions.astype(np.float64)[:, None] * frequency[None, :]
    cosine = np.cos(angles).astype(np.float32)
    sine = np.sin(angles).astype(np.float32)
    return jnp.asarray(np.concatenate([cosine, cosine], 1)), jnp.asarray(np.concatenate([-sine, sine], 1))


def solution(mesh):
    def shards(clean_states, noise_mask, mask_embed, queries, w_key, w_value):
        _, rows, width = clean_states.shape
        cosine, sine = tables_of(np.arange(2 * rows))
        far_cosine, far_sine = tables_of(np.arange(8) * 2 * rows)
        any_ = pl.BlockSpec(memory_space=pl.ANY)
        vmem = pl.BlockSpec(memory_space=pltpu.VMEM)
        output = pl.pallas_call(
            kernel,
            out_shape=jax.ShapeDtypeStruct((256, 2048), BF16),
            in_specs=[any_, vmem, vmem, any_, any_, any_, any_, any_, vmem, vmem],
            out_specs=any_,
            scratch_shapes=[
                pltpu.VMEM((528, 4096), BF16),
                pltpu.VMEM((32, 128, 512), BF16),
                pltpu.VMEM((528, 512), F32),
                pltpu.VMEM((2, 512, 128), BF16),
                pltpu.VMEM((2, 512, 128), BF16),
                pltpu.VMEM((8192, 128), BF16),
                pltpu.VMEM((8192, 256), BF16),
                pltpu.VMEM((4, 256, 512), BF16),
                pltpu.VMEM((4, 256, 128), BF16),
                pltpu.VMEM((4, 256, 512), BF16),
                pltpu.VMEM((4, 512, 128), F32),
                pltpu.VMEM((16, 256, 128), F32),
                pltpu.VMEM((16, 256, 256), F32),
                pltpu.SemaphoreType.DMA((EV_COUNT,)),
                pltpu.SemaphoreType.DMA((EV_COUNT,)),
                pltpu.SemaphoreType.DMA((10,)),
            ],
            compiler_params=pltpu.CompilerParams(
                collective_id=0, has_side_effects=True, vmem_limit_bytes=56 << 20
            ),
        )(
            clean_states[0], noise_mask, mask_embed[None, :], queries[0],
            w_key, w_value, cosine, sine, far_cosine, far_sine,
        )
        return output[None]

    placed = (
        P("fsdp", "seq", None),
        P("fsdp", "seq"),
        P(),
        P("fsdp", "seq", None),
        P("fsdp", None),
        P("fsdp", None),
    )
    return jax.shard_map(
        shards, mesh=mesh, in_specs=placed, out_specs=P("fsdp", "seq", None), check_vma=False
    )
```

time: 422 us -> 88.4 us (0.21)
  waiting for transfers between devices: 273 us -> 0 us
  Pallas kernels: 0 us -> 84.5 us
  local copies, waits for them, and re-layouts: 62 us -> 3.62 us
  matrix products: 46.7 us -> 0 us
  other arithmetic: 22.8 us -> 0 us
  between operations: 13.3 us -> 0.01 us
    all_gather x4 -> x0, waiting for transfers between devices: 271 us -> none  [the longest x1 99.3 us: shards(): lax.all_gather(w_value, 'fsdp', axis=0, tiled=True)]
    pallas_call x0 -> x1, Pallas kernels: none -> 84.5 us  [shards(): pl.pallas_call(kernel, out_shape=jax.ShapeDtypeStruct((256, 2048), BF16),...]
    dot_general x36 -> x0, matrix products: 46.7 us -> none  [the longest x17 24.7 us: absorb(): jnp.einsum('qkgt,tkd->qkgd', weights.astype(jnp.bfloat16), value_part.res...]
    dynamic_slice x48 -> x0, local copies, waits for them, and re-layouts: 33.3 us -> none  [the longest x32 17.7 us: sub_step(): value_part = lax.dynamic_slice_in_dim(value_stack, offset, BLOCK, 0)]
    while x80 -> x0, local copies, waits for them, and re-layouts: 21.8 us -> none
    reduce_sum x17 -> x0, other arithmetic: 17.4 us -> none  [absorb(): row_sum = row_sum * rescale + jnp.sum(weights, -1)]
  transfers between devices with their start and end apart: 4 -> 0, of which waited for: 4 -> 0; matrix products, arithmetic and copies ran while one was open for 5% -> 0% of each run, Pallas kernels for 0% -> 0%
where the time goes in v1:
time: 88.4 us; the launch traced here: 88.1 us
  Pallas kernels  84.5 us (96%)
  local copies, waits for them, and re-layouts  3.62 us (4%)
    pallas_call x1, Pallas kernels, shards(): pl.pallas_call(kernel, out_shape=jax.ShapeDtypeStruct((256, 2048), BF16),...  84.5 us
    unnamed x1, local copies, waits for them, and re-layouts  2.3 us

profile of v1, /device:TPU:3, one launch (start us, length us, event | category | flops | bytes accessed | tf_op | source)
XLA Modules:
  0.0 88.1 jit_solution(9948768660440949669)
XLA Ops:
  0.0 1.3 %broadcast_in_dim.6.mask_row = bf16[1,4096]{1,0:T(2,128)(2,1)} reshape(bf16[4096]{0:T(1024)(128)(2,1)} %param.12) | data formatting | bytes 16384 | tf_op jit(solution)/shard_map/broadcast_in_dim | solution.py:448
  1.3 84.5 %shard_map.100 = bf16[256,2048]{1,0:T(8,128)(2,1)} custom-call(bf16[256,4096]{1,0:T(8,128)(2,1)} %bitcast.4, s32[1,256]{1,0:T(1,128)} %marks.1, bf16[1,4096]{1,0:T(2,128)(2,1)} %broadcast_in_dim.6.mask_row, bf16[256,2048]{1,0:T(8,128)(2,1)} %bitcast.5, bf16[256,512]{1,0:T(8,128)(2,1)} %w_key.1, bf16[256,512]{1,0:T(8,128)(2,1)} %w_value.1, ...), custom_call_target="tpu_custom_call" | custom-call | tf_op jit(solution)/shard_map/pallas_call | solution.py:421
  85.8 2.3 %copy.12 = bf16[1,256,2048]{2,1,0:T(8,128)(2,1)} copy(bf16[1,256,2048]{2,1,0:T(8,128)(2,1)} %bitcast.3) | data formatting | bytes 2097152

commit v2 on v1

--- a/solution.py
+++ b/solution.py
@@ -16,13 +16,12 @@
 NT = (((1,), (1,)), ((), ()))
 
 ROUTE = {
-    (0, 1, 0): "y+", (0, 1, 1): "y-", (1, 1, 0): "xl", (1, 1, 1): "y+",
-    (0, 2, 0): "y-", (0, 2, 1): "xl", (1, 2, 0): "xh", (1, 2, 1): "xh",
-    (0, 3, 0): "y+", (0, 3, 1): "y-", (1, 3, 0): "xl", (1, 3, 1): "y+",
-    (0, 4, 0): "y-", (0, 4, 1): "xl", (1, 4, 0): "y-", (1, 4, 1): "xl",
+    (0, 1, 0): "buddy", (0, 1, 1): "xl", (1, 1, 0): "buddy", (1, 1, 1): "xl",
+    (0, 2, 0): "buddy", (0, 2, 1): "xl", (1, 2, 0): "xh", (1, 2, 1): "xh",
+    (0, 3, 0): "buddy", (0, 3, 1): "xl", (1, 3, 0): "mate", (1, 3, 1): "xl",
+    (0, 4, 0): "buddy", (0, 4, 1): "xl", (1, 4, 0): "mate", (1, 4, 1): "buddy",
 }
-OPPOSITE = {"y+": "y-", "y-": "y+", "xl": "xl", "xh": "xh"}
-KV_ORDER = ((0, 1), (1, 0), (3, 0), (1, 1), (3, 1), (2, 0), (2, 1))
+PLANE = ((0, 1), (1, 0), (3, 0), (1, 1), (3, 1), (2, 0), (2, 1))
 
 EV_X, EV_XH, EV_Z, EV_P = 0, 1, 3, 19
 EV_Q, EV_M, EV_K, EV_V, EV_O = 35, 38, 41, 49, 57
@@ -35,7 +34,7 @@
 
 def kernel(
     states, marks, mask_row, queries, w_key, w_value, cosine, sine, far_cosine, far_sine, out,
-    x_buf, w_buf, sums, k_own, v_own, k_all, v_all, q_buf, m_buf, o_buf,
+    x_buf, w_buf, sums, k_own, v_own, v_relay, k_all, v_all, q_buf, m_buf, o_buf,
     tables, row_max, mix, send_sem, recv_sem, local_sem,
 ):
     seq = lax.axis_index("seq")
@@ -54,8 +53,7 @@
         return ((yy % 4 * 2 + xx) * 2 + cc, fsdp)
 
     near = {
-        "y+": at(y + 1, xl, core),
-        "y-": at(y + 3, xl, core),
+        "buddy": at(y // 2 * 2 + 1 - y % 2, xl, core),
         "xl": at(y, 1 - xl, core),
         "xh": (at(y, 1 - xl, core)[0], z * 2 + 1 - xh),
         "z+": (seq, (z + 1) % 8 * 2 + xh),
@@ -94,7 +92,7 @@
     for number, table in enumerate((cosine, sine)):
         load_t.append(local(table, tables.at[number], 6 + number))
 
-    peers = [at(y + dy, xl if dx == 0 else 1 - xl, core) for dy, dx in KV_ORDER]
+    peers = [at(y + dy, xl if dx == 0 else 1 - xl, core) for dy, dx in PLANE]
     peers += [near["core"], near["mate2"], near["xh"], near["z+"], near["z-"]]
     barrier = pltpu.get_barrier_semaphore()
     for peer in peers:
@@ -132,7 +130,10 @@
     send(w_buf.at[own + side], w_buf.at[own + side], EV_XH + 1, near["xh"])
     send(states, x_buf.at[my_rows, :], EV_X, near["core"])
 
-    x_buf[pl.ds(512, 16), :] = jnp.broadcast_to(mask_row[...], (16, mask_row.shape[1]))
+    mask_rows = mask_row[...].astype(F32)
+    for i in range(32):
+        wide_row = jnp.broadcast_to(mask_rows[i : i + 1, :], (16, 128))
+        x_buf[pl.ds(512, 16), pl.ds(i * 128, 128)] = wide_row.astype(BF16)
     flags = jnp.broadcast_to(marks[...].astype(F32), (128, 256))
     m_buf[core] = jnp.transpose(flags).astype(BF16)
     v_all[:, pl.ds(128, 128)] = jnp.ones((v_all.shape[0], 128), BF16)
@@ -184,7 +185,7 @@
             for flip in range(2):
                 way = ROUTE[ring, distance, flip]
                 ref = w_buf.at[piece(source + 8, flip, 1 - side), part(distance, ring), :]
-                remote(ref, ref, EV_P + event(ring, distance, flip), near[OPPOSITE[way]]).wait_recv()
+                remote(ref, ref, EV_P + event(ring, distance, flip), near[way]).wait_recv()
 
     for distance in range(1, 5):
         for flip in range(2):
@@ -231,11 +232,38 @@
     def v_at(where):
         return v_all.at[kv_rows(where), pl.ds(0, 128)]
 
-    for dy, dx in KV_ORDER:
-        device = at(y + dy, xl if dx == 0 else 1 - xl, core)
+    beside = y * 2 + 1 - xl
+
+    def seen(dy, source_y):
+        return jnp.logical_not((source_y == 3) & ((dy == 2) | (dy == 3)))
+
+    def hop(dy):
+        return at(y + dy, xl, core)
+
+    send(v_own.at[1 - role], v_relay, EV_V, near["xl"])
+    send(k_own.at[role], k_at(chip), EV_K + 1, near["xl"])
+    send(v_own.at[role], v_at(chip), EV_V + 1, near["xl"])
+
+    def first_hop(dy, values):
         kind = (role + dy) % 2
-        send(k_own.at[kind], k_at(chip), EV_K + dy * 2 + dx, device)
-        send(v_own.at[kind], v_at(chip), EV_V + dy * 2 + dx, device)
+        if values:
+            return remote(v_own.at[kind], v_at(chip), EV_V + dy * 2, hop(dy))
+        return remote(k_own.at[kind], k_at(chip), EV_K + dy * 2, hop(dy))
+
+    def second_hop_v(dy):
+        source = v_at(beside) if dy == 2 else v_relay
+        return remote(source, v_at(beside), EV_V + dy * 2 + 1, hop(dy))
+
+    def second_hop_k(dy):
+        rows = k_at((y + 4 - dy) % 4 * 2 + xl)
+        return remote(rows, rows, EV_K + dy * 2 + 1, near["xl"])
+
+    for values in range(2):
+        for dy in (1, 3, 2):
+            @pl.when(seen(dy, y))
+            def _():
+                first_hop(dy, values).start()
+
     k_all[kv_rows(chip), :] = k_own[role]
     v_all[kv_rows(chip), pl.ds(0, 128)] = v_own[role]
 
@@ -254,133 +282,130 @@
     mask_key = jnp.broadcast_to(mask_key[0:1, :], (256, 128))
     mask_value = jnp.broadcast_to(mask_value[0:1, :], (256, 128)).astype(BF16).astype(F32)
 
-    def build(pair, quad):
+    def build(pair):
+        where = mate if pair else chip
         for i in range(2):
             slot = pair * 2 + i
-            mine = 2 * xl + i
-            base = 4096 + slot * 1024
-            block = pl.multiple_of((quad * 4 + mine) * 256, 256)
+            base = 4096 + slot * 512
+            block = pl.ds(pl.multiple_of(where * 512 + i * 256, 256), 256)
             masked = m_buf[slot].astype(F32) > 0.5
             noisy_k = jnp.where(
-                masked,
-                rotate(mask_key, pair, i * 256, 256),
-                k_all[pl.ds(block, 256), :].astype(F32),
+                masked, rotate(mask_key, pair, i * 256, 256), k_all[block, :].astype(F32)
             ).astype(BF16)
             noisy_v = jnp.where(
-                masked, mask_value, v_all[pl.ds(block, 256), pl.ds(0, 128)].astype(F32)
+                masked, mask_value, v_all[block, pl.ds(0, 128)].astype(F32)
             ).astype(BF16)
-            for j in range(4):
-                rows = pl.ds(base + j * 256, 256)
-                start = pl.multiple_of((quad * 4 + j) * 256, 256)
-
-                @pl.when(j < mine)
-                def _():
-                    k_all[rows, :] = k_all[pl.ds(start, 256), :]
-                    v_all[rows, pl.ds(0, 128)] = v_all[pl.ds(start, 256), pl.ds(0, 128)]
-
-                @pl.when(j >= mine)
-                def _():
-                    k_all[rows, :] = noisy_k
-
-                @pl.when(j == mine)
-                def _():
-                    v_all[rows, pl.ds(0, 128)] = noisy_v
-
-                @pl.when(j > mine)
-                def _():
-                    v_all[rows, :] = jnp.zeros((256, 256), BF16)
+            noisy = pl.ds(base + i * 256, 256)
+            k_all[noisy, :] = noisy_k
+            v_all[noisy, pl.ds(0, 128)] = noisy_v
+            if i == 0:
+                k_all[pl.ds(base + 256, 256), :] = noisy_k
+                v_all[pl.ds(base + 256, 256), :] = jnp.zeros((256, 256), BF16)
+            else:
+                before = pl.ds(pl.multiple_of(where * 512, 512), 256)
+                k_all[pl.ds(base, 256), :] = k_all[before, :]
+                v_all[pl.ds(base, 256), pl.ds(0, 128)] = v_all[before, pl.ds(0, 128)]
 
     def absorb(slot, start):
-        span = pl.ds(pl.multiple_of(start, 1024), 1024)
-        for g in range(4):
-            query = q_buf[slot, :, pl.ds(g * 128, 128)]
+        span = pl.ds(pl.multiple_of(start, 512), 512)
+        for tile in range(8):
+            query = q_buf[slot, pl.ds(tile % 2 * 128, 128), pl.ds(tile // 2 * 128, 128)]
             scores = lax.dot_general(query, k_all[span, :], NT, preferred_element_type=F32)
-            before = row_max[slot * 4 + g]
+            before = row_max[slot * 8 + tile]
             after = jnp.maximum(before, jnp.max(scores, 1, keepdims=True))
             shrink = jnp.exp2((before - after) * SCORE_SCALE)
-            probs = jnp.exp2((scores - after[:, :1]) * SCORE_SCALE).astype(BF16)
+            probs = jnp.exp2((scores - jnp.tile(after, (1, 4))) * SCORE_SCALE).astype(BF16)
             term = jnp.dot(probs, v_all[span, :], preferred_element_type=F32)
-            for part_ in range(2):
-                lanes = pl.ds(part_ * 128, 128)
-                mix[slot * 4 + g, :, lanes] = (
-                    mix[slot * 4 + g, :, lanes] * shrink + term[:, part_ * 128 : part_ * 128 + 128]
-                )
-            row_max[slot * 4 + g] = after
+            total = mix[slot * 8 + tile]
+            mix[slot * 8 + tile] = total * jnp.tile(shrink, (1, 2)) + term
+            row_max[slot * 8 + tile] = after
 
     def finish(slot):
-        for g in range(4):
-            total = mix[slot * 4 + g]
-            o_buf[slot, :, pl.ds(g * 128, 128)] = (total[:, :128] / total[:, 128:]).astype(BF16)
-
-    def wait_kv(source, dy, dx):
-        where = source * 2 + (xl if dx == 0 else 1 - xl)
-        device = at(source, xl if dx == 0 else 1 - xl, core)
-        remote(k_at(where), k_at(where), EV_K + dy * 2 + dx, device).wait_recv()
-        remote(v_at(where), v_at(where), EV_V + dy * 2 + dx, device).wait_recv()
-
-    def step(number, carry):
-        dy = jnp.where(number == 2, 3, number)
-        quad = (y + 4 - dy) % 4
-
-        @pl.when(number > 0)
-        def _():
-            wait_kv(quad, dy, 0)
-
-        wait_kv(quad, dy, 1)
+        for tile in range(8):
+            total = mix[slot * 8 + tile]
+            o_buf[slot, pl.ds(tile % 2 * 128, 128), pl.ds(tile // 2 * 128, 128)] = (
+                total[:, :128] / total[:, 128:]
+            ).astype(BF16)
+
+    out_cols = pl.ds(pl.multiple_of(head * 512, 512), 512)
+
+    def mate_out(i):
+        number = EV_O + (i - core + 2) % 2
+        return remote(o_buf.at[2 + i], out.at[:, out_cols], number, at(3 - y, xl, i))
+
+    late = (y == 0) | (y == 2)
+
+    def visit(number, carry):
+        turn = number % 8
+        first = number < 8
+        dy = jnp.where(turn < 2, 0, jnp.where(turn >= 6, 2, jnp.where(turn % 2 == 0, 1, 3)))
+        dx = jnp.where((turn == 1) | (turn == 4) | (turn == 5) | (turn == 7), 1, 0)
+        source_y = (y + 4 - dy) % 4
+        source = source_y * 2 + jnp.where(dx == 0, xl, 1 - xl)
+        here = seen(dy, source_y)
+        device = near["xl"]
+
+        @pl.when(number == 1)
+        def _():
+            remote(v_relay, v_relay, EV_V, device).wait_recv()
+            for hop_y in (1, 3):
+                @pl.when(seen(hop_y, y))
+                def _():
+                    second_hop_v(hop_y).start()
+            remote(v_at(beside), v_at(beside), EV_V + 1, device).wait_recv()
+
+            @pl.when(seen(2, y))
+            def _():
+                second_hop_v(2).start()
+
+        for hop_y, when in ((1, 2), (3, 2), (2, 4)):
+            @pl.when((number == when) & seen(hop_y, (y + 4 - hop_y) % 4))
+            def _():
+                rows = k_at((y + 4 - hop_y) % 4 * 2 + xl)
+                remote(rows, rows, EV_K + hop_y * 2, device).wait_recv()
+                second_hop_k(hop_y).start()
+
+        @pl.when(first & here & (dx == 1))
+        def _():
+            remote(k_at(source), k_at(source), EV_K + dy * 2 + 1, device).wait_recv()
+
+        @pl.when(first & here & (turn > 1))
+        def _():
+            remote(v_at(source), v_at(source), EV_V + dy * 2 + dx, device).wait_recv()
 
         @pl.when(number == 0)
         def _():
-            build(0, quad)
-
-        @pl.when(quad == 3 - y)
-        def _():
-            build(1, quad)
-
-        def item(kind, carry):
-            pair = jnp.where((kind == 1) | (kind == 2), 1, 0)
-            level = jnp.where(pair == 1, 3 - y, y)
-            active = jnp.where(kind < 2, quad == level, quad < level)
-
-            @pl.when(active)
+            build(0)
+
+        @pl.when(first & (source == mate))
+        def _():
+            build(1)
+
+        def item(slot, carry):
+            slot = (slot + 2) % 4
+            other_pair = slot >= 2
+            level = jnp.where(other_pair, mate, chip)
+            turn_now = jnp.where(other_pair | (y >= 2), first, jnp.logical_not(first))
+
+            @pl.when(turn_now & (source <= level))
             def _():
-                def one(i, carry):
-                    slot = pair * 2 + i
-                    absorb(slot, jnp.where(kind < 2, 4096 + slot * 1024, quad * 1024))
-                    return carry
-
-                lax.fori_loop(0, 2, one, 0)
+                absorb(slot, jnp.where(source == level, 4096 + slot * 512, source * 512))
 
             return carry
 
         lax.fori_loop(0, 4, item, 0)
+
+        @pl.when(number == jnp.where(late, 7, 5))
+        def _():
+            for i in range(2):
+                finish(2 + i)
+                mate_out(i).start()
+
         return carry
 
-    lax.fori_loop(0, 3, step, 0)
-
-    last = (y + 2) % 4
-    wait_kv(last, 2, 0)
-    wait_kv(last, 2, 1)
-    out_cols = pl.ds(pl.multiple_of(head * 512, 512), 512)
-
-    def final(i, carry):
-        slot = (i + 2) % 4
-
-        @pl.when(last < jnp.where(slot >= 2, 3 - y, y))
-        def _():
-            absorb(slot, last * 1024)
-
-        finish(slot)
-
-        @pl.when(slot >= 2)
-        def _():
-            remote(
-                o_buf.at[slot], out.at[:, out_cols], EV_O + (slot - core + 2) % 2,
-                at(3 - y, xl, slot % 2),
-            ).start()
-
-        return carry
-
-    lax.fori_loop(0, 4, final, 0)
+    lax.fori_loop(0, jnp.where(y < 2, 16, 8), visit, 0)
+    for i in range(2):
+        finish(i)
     send(o_buf.at[1 - core], out.at[:, out_cols], EV_O + 2, near["core"])
     store = local(o_buf.at[core], out.at[:, out_cols], 5)
     store.wait()
@@ -394,9 +419,18 @@
         (EV_O + 2, 2 * (1 - core) + role, near["core"]),
     ):
         remote(o_at(kv_head), o_at(kv_head), number, device).wait_recv()
-    for number in range(2):
-        slot = 2 + (core + number) % 2
-        remote(o_buf.at[slot], out.at[:, out_cols], EV_O + number, at(3 - y, xl, slot % 2)).wait_send()
+    for i in range(2):
+        mate_out(i).wait_send()
+    for dy in (1, 2, 3):
+        @pl.when(seen(dy, y))
+        def _():
+            for values in range(2):
+                first_hop(dy, values).wait_send()
+            second_hop_v(dy).wait_send()
+
+        @pl.when(seen(dy, (y + 4 - dy) % 4))
+        def _():
+            second_hop_k(dy).wait_send()
     for copy in sends:
         copy.wait_send()
 
@@ -422,21 +456,22 @@
             kernel,
             out_shape=jax.ShapeDtypeStruct((256, 2048), BF16),
             in_specs=[any_, vmem, vmem, any_, any_, any_, any_, any_, vmem, vmem],
-            out_specs=any_,
+            out_specs=vmem,
             scratch_shapes=[
                 pltpu.VMEM((528, 4096), BF16),
                 pltpu.VMEM((32, 128, 512), BF16),
                 pltpu.VMEM((528, 512), F32),
                 pltpu.VMEM((2, 512, 128), BF16),
                 pltpu.VMEM((2, 512, 128), BF16),
-                pltpu.VMEM((8192, 128), BF16),
-                pltpu.VMEM((8192, 256), BF16),
+                pltpu.VMEM((512, 128), BF16),
+                pltpu.VMEM((6144, 128), BF16),
+                pltpu.VMEM((6144, 256), BF16),
                 pltpu.VMEM((4, 256, 512), BF16),
                 pltpu.VMEM((4, 256, 128), BF16),
                 pltpu.VMEM((4, 256, 512), BF16),
                 pltpu.VMEM((4, 512, 128), F32),
-                pltpu.VMEM((16, 256, 128), F32),
-                pltpu.VMEM((16, 256, 256), F32),
+                pltpu.VMEM((32, 128, 128), F32),
+                pltpu.VMEM((32, 128, 256), F32),
                 pltpu.SemaphoreType.DMA((EV_COUNT,)),
                 pltpu.SemaphoreType.DMA((EV_COUNT,)),
                 pltpu.SemaphoreType.DMA((10,)),
@@ -445,7 +480,7 @@
                 collective_id=0, has_side_effects=True, vmem_limit_bytes=56 << 20
             ),
         )(
-            clean_states[0], noise_mask, mask_embed[None, :], queries[0],
+            clean_states[0], noise_mask, mask_embed.reshape(32, 128), queries[0],
             w_key, w_value, cosine, sine, far_cosine, far_sine,
         )
         return output[None]

time: 88.4 us -> 79.7 us (0.902)
  the two profiles are of different devices: /device:TPU:3 before, /device:TPU:79 now
where the time goes in v2:
time: 79.7 us; the launch traced here: 79.5 us
  Pallas kernels  77.2 us (97%)
  local copies, waits for them, and re-layouts  2.3 us (3%)
    pallas_call x1, Pallas kernels, shards(): pl.pallas_call(kernel, out_shape=jax.ShapeDtypeStruct((256, 2048), BF16),...  77.2 us
    unnamed x1, local copies, waits for them, and re-layouts  2.3 us

profile of v2, /device:TPU:79, one launch (start us, length us, event | category | flops | bytes accessed | tf_op | source)
XLA Modules:
  0.0 79.5 jit_solution(12176190771547431305)
XLA Ops:
  0.0 77.2 %shard_map.100 = bf16[256,2048]{1,0:T(8,128)(2,1)} custom-call(bf16[256,4096]{1,0:T(8,128)(2,1)} %bitcast.5, s32[1,256]{1,0:T(1,128)} %marks.1, bf16[32,128]{1,0:T(8,128)(2,1)} %bitcast.7, bf16[256,2048]{1,0:T(8,128)(2,1)} %bitcast.6, bf16[256,512]{1,0:T(8,128)(2,1)} %w_key.1, bf16[256,512]{1,0:T(8,128)(2,1)} %w_value.1, f32[512,128]{1,0:T(8,128)} %constant.8.clone.cosine, ...), custom_call_target="tpu_custom_call" | custom-call | tf_op jit(solution)/shard_map/pallas_call | solution.py:455
  77.2 2.3 %copy.12 = bf16[1,256,2048]{2,1,0:T(8,128)(2,1)} copy(bf16[1,256,2048]{2,1,0:T(8,128)(2,1)} %bitcast.4) | data formatting | bytes 2097152

commit v3 on v2

--- a/solution.py
+++ b/solution.py
@@ -130,29 +130,14 @@
     send(w_buf.at[own + side], w_buf.at[own + side], EV_XH + 1, near["xh"])
     send(states, x_buf.at[my_rows, :], EV_X, near["core"])
 
-    mask_rows = mask_row[...].astype(F32)
-    for i in range(32):
-        wide_row = jnp.broadcast_to(mask_rows[i : i + 1, :], (16, 128))
-        x_buf[pl.ds(512, 16), pl.ds(i * 128, 128)] = wide_row.astype(BF16)
-    flags = jnp.broadcast_to(marks[...].astype(F32), (128, 256))
-    m_buf[core] = jnp.transpose(flags).astype(BF16)
-    v_all[:, pl.ds(128, 128)] = jnp.ones((v_all.shape[0], 128), BF16)
-    row_max[...] = jnp.full(row_max.shape, -1e30, F32)
-    mix[...] = jnp.zeros(mix.shape, F32)
-
-    for copy in load_t:
-        copy.wait()
-    near_c, near_s = tables[0], tables[1]
-    for pair, where in ((1, mate), (0, chip)):
-        far_c, far_s = far_cosine[pl.ds(where, 1), :], far_sine[pl.ds(where, 1), :]
-        tables[pair * 2] = near_c * far_c - near_s * far_s
-        tables[pair * 2 + 1] = near_s * far_c + near_c * far_s
-
     landing = w_buf.at[other + side]
     remote(landing, landing, EV_XH, near["xh"]).wait_recv()
     for ring in range(2):
         ring_send(ring, 1, 1)
 
+    flags = jnp.broadcast_to(marks[...].astype(F32), (128, 256))
+    m_buf[core] = jnp.transpose(flags).astype(BF16)
+
     def q_at(kv_head):
         return queries.at[:, pl.ds(pl.multiple_of(kv_head * 512, 512), 512)]
 
@@ -160,12 +145,6 @@
     send(m_buf.at[core], m_buf.at[core], EV_M, near["core"])
     send(m_buf.at[core], m_buf.at[2 + core], EV_M + 1, near["mate"])
     send(m_buf.at[core], m_buf.at[2 + core], EV_M + 2, near["mate2"])
-
-    load_x.wait()
-    theirs = x_buf.at[pl.ds(pl.multiple_of((1 - core) * 256, 256), 256), :]
-    remote(theirs, theirs, EV_X, near["core"]).wait_recv()
-    landing = w_buf.at[other + 1 - side]
-    remote(landing, landing, EV_XH + 1, near["xh"]).wait_recv()
 
     def project(zz, first=False):
         zz = zz % 8
@@ -176,8 +155,6 @@
             sums[...] = term
         else:
             sums[...] += term
-
-    project(z, True)
 
     def plane_wait(distance):
         for ring in range(2):
@@ -204,6 +181,27 @@
                         ref = w_buf.at[piece(source + 8, 1 - mine, side), part(distance, ring), :]
                         send(ref, ref, EV_P + event(ring, distance, mine), near["xh"])
         if distance == 1:
+            mask_rows = mask_row[...].astype(F32)
+            for i in range(32):
+                wide_row = jnp.broadcast_to(mask_rows[i : i + 1, :], (16, 128))
+                x_buf[pl.ds(512, 16), pl.ds(i * 128, 128)] = wide_row.astype(BF16)
+            v_all[:, pl.ds(128, 128)] = jnp.ones((v_all.shape[0], 128), BF16)
+            row_max[...] = jnp.full(row_max.shape, -1e30, F32)
+            mix[...] = jnp.zeros(mix.shape, F32)
+
+            for copy in load_t:
+                copy.wait()
+            near_c, near_s = tables[0], tables[1]
+            for pair, where in ((1, mate), (0, chip)):
+                far_c, far_s = far_cosine[pl.ds(where, 1), :], far_sine[pl.ds(where, 1), :]
+                tables[pair * 2] = near_c * far_c - near_s * far_s
+                tables[pair * 2 + 1] = near_s * far_c + near_c * far_s
+            load_x.wait()
+            theirs = x_buf.at[pl.ds(pl.multiple_of((1 - core) * 256, 256), 256), :]
+            remote(theirs, theirs, EV_X, near["core"]).wait_recv()
+            landing = w_buf.at[other + 1 - side]
+            remote(landing, landing, EV_XH + 1, near["xh"]).wait_recv()
+            project(z, True)
             send(q_at(2 * core + 1 - role), q_buf.at[2 + core], EV_Q + 1, near["mate"])
             send(q_at(2 * (1 - core) + 1 - role), q_buf.at[2 + core], EV_Q + 2, near["mate2"])
         else:
@@ -258,11 +256,10 @@
         rows = k_at((y + 4 - dy) % 4 * 2 + xl)
         return remote(rows, rows, EV_K + dy * 2 + 1, near["xl"])
 
-    for values in range(2):
-        for dy in (1, 3, 2):
-            @pl.when(seen(dy, y))
-            def _():
-                first_hop(dy, values).start()
+    for dy, values in ((1, 0), (3, 0), (1, 1), (3, 1), (2, 0), (2, 1)):
+        @pl.when(seen(dy, y))
+        def _():
+            first_hop(dy, values).start()
 
     k_all[kv_rows(chip), :] = k_own[role]
     v_all[kv_rows(chip), pl.ds(0, 128)] = v_own[role]
@@ -335,41 +332,50 @@
 
     late = (y == 0) | (y == 2)
 
+    def source_of(turn):
+        dy = jnp.where(turn >= 6, 2, jnp.where((turn == 0) | (turn == 3), 0, jnp.where((turn == 1) | (turn == 4), 1, 3)))
+        dx = jnp.where((turn == 3) | (turn == 4) | (turn == 5) | (turn == 7), 1, 0)
+        source_y = (y + 4 - dy) % 4
+        return dy, dx, source_y, source_y * 2 + jnp.where(dx == 0, xl, 1 - xl)
+
     def visit(number, carry):
         turn = number % 8
         first = number < 8
-        dy = jnp.where(turn < 2, 0, jnp.where(turn >= 6, 2, jnp.where(turn % 2 == 0, 1, 3)))
-        dx = jnp.where((turn == 1) | (turn == 4) | (turn == 5) | (turn == 7), 1, 0)
-        source_y = (y + 4 - dy) % 4
-        source = source_y * 2 + jnp.where(dx == 0, xl, 1 - xl)
-        here = seen(dy, source_y)
+        dy, dx, source_y, source = source_of(turn)
+        here = first & seen(dy, source_y)
         device = near["xl"]
 
-        @pl.when(number == 1)
-        def _():
-            remote(v_relay, v_relay, EV_V, device).wait_recv()
-            for hop_y in (1, 3):
-                @pl.when(seen(hop_y, y))
-                def _():
-                    second_hop_v(hop_y).start()
-            remote(v_at(beside), v_at(beside), EV_V + 1, device).wait_recv()
-
-            @pl.when(seen(2, y))
-            def _():
-                second_hop_v(2).start()
-
-        for hop_y, when in ((1, 2), (3, 2), (2, 4)):
-            @pl.when((number == when) & seen(hop_y, (y + 4 - hop_y) % 4))
+        def pass_on_k(hop_y):
+            @pl.when(seen(hop_y, (y + 4 - hop_y) % 4))
             def _():
                 rows = k_at((y + 4 - hop_y) % 4 * 2 + xl)
                 remote(rows, rows, EV_K + hop_y * 2, device).wait_recv()
                 second_hop_k(hop_y).start()
 
-        @pl.when(first & here & (dx == 1))
+        def pass_on_v(hop_y):
+            @pl.when(seen(hop_y, y))
+            def _():
+                second_hop_v(hop_y).start()
+
+        @pl.when(number == 1)
+        def _():
+            remote(v_relay, v_relay, EV_V, device).wait_recv()
+            pass_on_v(1)
+            pass_on_v(3)
+            pass_on_k(1)
+            pass_on_k(3)
+
+        @pl.when(number == 3)
+        def _():
+            remote(v_at(beside), v_at(beside), EV_V + 1, device).wait_recv()
+            pass_on_v(2)
+            pass_on_k(2)
+
+        @pl.when(here & (dx == 1))
         def _():
             remote(k_at(source), k_at(source), EV_K + dy * 2 + 1, device).wait_recv()
 
-        @pl.when(first & here & (turn > 1))
+        @pl.when(here & (turn != 0) & (turn != 3))
         def _():
             remote(v_at(source), v_at(source), EV_V + dy * 2 + dx, device).wait_recv()
 
@@ -381,26 +387,29 @@
         def _():
             build(1)
 
-        def item(slot, carry):
-            slot = (slot + 2) % 4
+        def item(index, carry):
+            both = turn == 7
+            slot = (jnp.where(both, index // 2, index) + 2) % 4
+            _, _, _, earlier = source_of(6)
+            origin = jnp.where(both & (index % 2 == 0), earlier, source)
             other_pair = slot >= 2
             level = jnp.where(other_pair, mate, chip)
             turn_now = jnp.where(other_pair | (y >= 2), first, jnp.logical_not(first))
 
-            @pl.when(turn_now & (source <= level))
+            @pl.when(turn_now & (origin <= level))
             def _():
-                absorb(slot, jnp.where(source == level, 4096 + slot * 512, source * 512))
+                absorb(slot, jnp.where(origin == level, 4096 + slot * 512, origin * 512))
+
+            done = number == jnp.where(late, 7, 5)
+
+            @pl.when(other_pair & done & ((turn < 7) | (index % 2 == 1)))
+            def _():
+                finish(slot)
+                mate_out(slot - 2).start()
 
             return carry
 
-        lax.fori_loop(0, 4, item, 0)
-
-        @pl.when(number == jnp.where(late, 7, 5))
-        def _():
-            for i in range(2):
-                finish(2 + i)
-                mate_out(i).start()
-
+        lax.fori_loop(0, jnp.where(turn < 6, 4, jnp.where(turn == 6, 0, 8)), item, 0)
         return carry
 
     lax.fori_loop(0, jnp.where(y < 2, 16, 8), visit, 0)

time: 79.7 us -> 74.1 us (0.930)
  the two profiles are of different devices: /device:TPU:79 before, /device:TPU:3 now
where the time goes in v3:
time: 74.1 us; the launch traced here: 74 us
  Pallas kernels  71.7 us (97%)
  local copies, waits for them, and re-layouts  2.3 us (3%)
    pallas_call x1, Pallas kernels, shards(): pl.pallas_call(kernel, out_shape=jax.ShapeDtypeStruct((256, 2048), BF16),...  71.7 us
    unnamed x1, local copies, waits for them, and re-layouts  2.3 us

profile of v3, /device:TPU:3, one launch (start us, length us, event | category | flops | bytes accessed | tf_op | source)
XLA Modules:
  0.0 74.0 jit_solution(5500077257637078728)
XLA Ops:
  0.0 71.7 %shard_map.100 = bf16[256,2048]{1,0:T(8,128)(2,1)} custom-call(bf16[256,4096]{1,0:T(8,128)(2,1)} %bitcast.5, s32[1,256]{1,0:T(1,128)} %marks.1, bf16[32,128]{1,0:T(8,128)(2,1)} %bitcast.7, bf16[256,2048]{1,0:T(8,128)(2,1)} %bitcast.6, bf16[256,512]{1,0:T(8,128)(2,1)} %w_key.1, bf16[256,512]{1,0:T(8,128)(2,1)} %w_value.1, f32[512,128]{1,0:T(8,128)} %constant.8.clone.cosine, ...), custom_call_target="tpu_custom_call" | custom-call | tf_op jit(solution)/shard_map/pallas_call | solution.py:464
  71.7 2.3 %copy.12 = bf16[1,256,2048]{2,1,0:T(8,128)(2,1)} copy(bf16[1,256,2048]{2,1,0:T(8,128)(2,1)} %bitcast.4) | data formatting | bytes 2097152

commit v4 on v3

--- a/solution.py
+++ b/solution.py
@@ -463,7 +463,7 @@
         vmem = pl.BlockSpec(memory_space=pltpu.VMEM)
         output = pl.pallas_call(
             kernel,
-            out_shape=jax.ShapeDtypeStruct((256, 2048), BF16),
+            out_shape=pltpu.VMEM((256, 2048), BF16),
             in_specs=[any_, vmem, vmem, any_, any_, any_, any_, any_, vmem, vmem],
             out_specs=vmem,
             scratch_shapes=[

time: 74.1 us -> 71.8 us (0.969)
  local copies, waits for them, and re-layouts: 2.3 us -> 0.97 us
  Pallas kernels: 71.7 us -> 70.7 us
    unnamed x1, local copies, waits for them, and re-layouts: 2.3 us -> 0.97 us
    pallas_call x1, Pallas kernels: 71.7 us -> 70.7 us  [shards(): pl.pallas_call(kernel, out_shape=pltpu.VMEM((256, 2048), BF16), in_specs=...]
where the time goes in v4:
time: 71.8 us; the launch traced here: 71.6 us
  Pallas kernels  70.7 us (98%)
  local copies, waits for them, and re-layouts  0.97 us (1%)
    pallas_call x1, Pallas kernels, shards(): pl.pallas_call(kernel, out_shape=pltpu.VMEM((256, 2048), BF16), in_specs=...  70.7 us

profile of v4, /device:TPU:3, one launch (start us, length us, event | category | flops | bytes accessed | tf_op | source)
XLA Modules:
  0.0 71.6 jit_solution(15809874229462211984)
XLA Ops:
  0.0 70.7 %shard_map.100 = bf16[256,2048]{1,0:T(8,128)(2,1)S(1)} custom-call(bf16[256,4096]{1,0:T(8,128)(2,1)} %bitcast.5, s32[1,256]{1,0:T(1,128)} %marks.1, bf16[32,128]{1,0:T(8,128)(2,1)} %bitcast.7, bf16[256,2048]{1,0:T(8,128)(2,1)} %bitcast.6, bf16[256,512]{1,0:T(8,128)(2,1)} %w_key.1, bf16[256,512]{1,0:T(8,128)(2,1)} %w_value.1, ...), custom_call_target="tpu_custom_call" | custom-call | tf_op jit(solution)/shard_map/pallas_call | solution.py:464
  70.7 1.0 %copy.12 = bf16[1,256,2048]{2,1,0:T(8,128)(2,1)} copy(bf16[1,256,2048]{2,1,0:T(8,128)(2,1)S(1)} %bitcast.4) | data formatting | bytes 2097152

commit v5 on v4

--- a/solution.py
+++ b/solution.py
@@ -185,9 +185,6 @@
             for i in range(32):
                 wide_row = jnp.broadcast_to(mask_rows[i : i + 1, :], (16, 128))
                 x_buf[pl.ds(512, 16), pl.ds(i * 128, 128)] = wide_row.astype(BF16)
-            v_all[:, pl.ds(128, 128)] = jnp.ones((v_all.shape[0], 128), BF16)
-            row_max[...] = jnp.full(row_max.shape, -1e30, F32)
-            mix[...] = jnp.zeros(mix.shape, F32)
 
             for copy in load_t:
                 copy.wait()
@@ -208,6 +205,10 @@
             plane_wait(distance - 1)
             project(z + 8 - distance + 1)
             project(z + distance - 1)
+            if distance == 3:
+                v_all[:, pl.ds(128, 128)] = jnp.ones((v_all.shape[0], 128), BF16)
+                row_max[...] = jnp.full(row_max.shape, -1e30, F32)
+                mix[...] = jnp.zeros(mix.shape, F32)
     plane_wait(4)
     project(z + 4)
 

time: 71.8 us -> 71.8 us (level)
  no operation moved by 1% of the time
where the time goes in v5:
time: 71.8 us; the launch traced here: 71.6 us
  Pallas kernels  70.7 us (98%)
  local copies, waits for them, and re-layouts  0.97 us (1%)
    pallas_call x1, Pallas kernels, shards(): pl.pallas_call(kernel, out_shape=pltpu.VMEM((256, 2048), BF16), in_specs=...  70.7 us

profile of v5, /device:TPU:3, one launch (start us, length us, event | category | flops | bytes accessed | tf_op | source)
XLA Modules:
  0.0 71.6 jit_solution(15281117262461918409)
XLA Ops:
  0.0 70.7 %shard_map.100 = bf16[256,2048]{1,0:T(8,128)(2,1)S(1)} custom-call(bf16[256,4096]{1,0:T(8,128)(2,1)} %bitcast.5, s32[1,256]{1,0:T(1,128)} %marks.1, bf16[32,128]{1,0:T(8,128)(2,1)} %bitcast.7, bf16[256,2048]{1,0:T(8,128)(2,1)} %bitcast.6, bf16[256,512]{1,0:T(8,128)(2,1)} %w_key.1, bf16[256,512]{1,0:T(8,128)(2,1)} %w_value.1, ...), custom_call_target="tpu_custom_call" | custom-call | tf_op jit(solution)/shard_map/pallas_call | solution.py:465
  70.7 1.0 %copy.12 = bf16[1,256,2048]{2,1,0:T(8,128)(2,1)} copy(bf16[1,256,2048]{2,1,0:T(8,128)(2,1)S(1)} %bitcast.4) | data formatting | bytes 2097152

commit v6 on v5

--- a/solution.py
+++ b/solution.py
@@ -217,29 +217,29 @@
         span = pl.ds(first, count)
         return rows * tables[pair * 2, span, :] + turned * tables[pair * 2 + 1, span, :]
 
+    def kv_rows(where):
+        return pl.ds(pl.multiple_of(where * 512, 512), 512)
+
+    def k_at(where):
+        return k_all.at[kv_rows(where), :]
+
+    def v_at(where):
+        return v_all.at[kv_rows(where), pl.ds(0, 128)]
+
+    beside = y * 2 + 1 - xl
+
+    def seen(dy, source_y):
+        return jnp.logical_not((source_y == 3) & ((dy == 2) | (dy == 3)))
+
+    def hop(dy):
+        return at(y + dy, xl, core)
+
+    for kind in range(2):
+        v_own[kind] = sums[pl.ds(0, 512), pl.ds(256 + kind * 128, 128)].astype(BF16)
+    send(v_own.at[1 - role], v_relay, EV_V, near["xl"])
     for kind in range(2):
         keys = sums[pl.ds(0, 512), pl.ds(kind * 128, 128)]
         k_own[kind] = rotate(keys, 0, 0, 512).astype(BF16)
-        v_own[kind] = sums[pl.ds(0, 512), pl.ds(256 + kind * 128, 128)].astype(BF16)
-
-    def kv_rows(where):
-        return pl.ds(pl.multiple_of(where * 512, 512), 512)
-
-    def k_at(where):
-        return k_all.at[kv_rows(where), :]
-
-    def v_at(where):
-        return v_all.at[kv_rows(where), pl.ds(0, 128)]
-
-    beside = y * 2 + 1 - xl
-
-    def seen(dy, source_y):
-        return jnp.logical_not((source_y == 3) & ((dy == 2) | (dy == 3)))
-
-    def hop(dy):
-        return at(y + dy, xl, core)
-
-    send(v_own.at[1 - role], v_relay, EV_V, near["xl"])
     send(k_own.at[role], k_at(chip), EV_K + 1, near["xl"])
     send(v_own.at[role], v_at(chip), EV_V + 1, near["xl"])
 

time: 71.8 us -> 72 us (level)
  no operation moved by 1% of the time
where the time goes in v6:
time: 72 us; the launch traced here: 71.8 us
  Pallas kernels  70.9 us (98%)
  local copies, waits for them, and re-layouts  0.97 us (1%)
    pallas_call x1, Pallas kernels, shards(): pl.pallas_call(kernel, out_shape=pltpu.VMEM((256, 2048), BF16), in_specs=...  70.9 us

profile of v6, /device:TPU:3, one launch (start us, length us, event | category | flops | bytes accessed | tf_op | source)
XLA Modules:
  0.0 71.8 jit_solution(9791280926077927141)
XLA Ops:
  0.0 70.9 %shard_map.100 = bf16[256,2048]{1,0:T(8,128)(2,1)S(1)} custom-call(bf16[256,4096]{1,0:T(8,128)(2,1)} %bitcast.5, s32[1,256]{1,0:T(1,128)} %marks.1, bf16[32,128]{1,0:T(8,128)(2,1)} %bitcast.7, bf16[256,2048]{1,0:T(8,128)(2,1)} %bitcast.6, bf16[256,512]{1,0:T(8,128)(2,1)} %w_key.1, bf16[256,512]{1,0:T(8,128)(2,1)} %w_value.1, ...), custom_call_target="tpu_custom_call" | custom-call | tf_op jit(solution)/shard_map/pallas_call | solution.py:465
  70.9 1.0 %copy.12 = bf16[1,256,2048]{2,1,0:T(8,128)(2,1)} copy(bf16[1,256,2048]{2,1,0:T(8,128)(2,1)S(1)} %bitcast.4) | data formatting | bytes 2097152

commit v7 on v5

--- a/solution.py
+++ b/solution.py
@@ -19,7 +19,7 @@
     (0, 1, 0): "buddy", (0, 1, 1): "xl", (1, 1, 0): "buddy", (1, 1, 1): "xl",
     (0, 2, 0): "buddy", (0, 2, 1): "xl", (1, 2, 0): "xh", (1, 2, 1): "xh",
     (0, 3, 0): "buddy", (0, 3, 1): "xl", (1, 3, 0): "mate", (1, 3, 1): "xl",
-    (0, 4, 0): "buddy", (0, 4, 1): "xl", (1, 4, 0): "mate", (1, 4, 1): "buddy",
+    (0, 4, 0): "buddy", (0, 4, 1): "xl", (1, 4, 0): "xh", (1, 4, 1): "xh",
 }
 PLANE = ((0, 1), (1, 0), (3, 0), (1, 1), (3, 1), (2, 0), (2, 1))
 

time: 71.8 us -> 71.7 us (level)
  no operation moved by 1% of the time
where the time goes in v7:
time: 71.7 us; the launch traced here: 71.5 us
  Pallas kernels  70.5 us (98%)
  local copies, waits for them, and re-layouts  0.97 us (1%)
    pallas_call x1, Pallas kernels, shards(): pl.pallas_call(kernel, out_shape=pltpu.VMEM((256, 2048), BF16), in_specs=...  70.5 us

profile of v7, /device:TPU:3, one launch (start us, length us, event | category | flops | bytes accessed | tf_op | source)
XLA Modules:
  0.0 71.5 jit_solution(11017017183421382392)
XLA Ops:
  0.0 70.5 %shard_map.100 = bf16[256,2048]{1,0:T(8,128)(2,1)S(1)} custom-call(bf16[256,4096]{1,0:T(8,128)(2,1)} %bitcast.5, s32[1,256]{1,0:T(1,128)} %marks.1, bf16[32,128]{1,0:T(8,128)(2,1)} %bitcast.7, bf16[256,2048]{1,0:T(8,128)(2,1)} %bitcast.6, bf16[256,512]{1,0:T(8,128)(2,1)} %w_key.1, bf16[256,512]{1,0:T(8,128)(2,1)} %w_value.1, ...), custom_call_target="tpu_custom_call" | custom-call | tf_op jit(solution)/shard_map/pallas_call | solution.py:465
  70.5 1.0 %copy.12 = bf16[1,256,2048]{2,1,0:T(8,128)(2,1)} copy(bf16[1,256,2048]{2,1,0:T(8,128)(2,1)S(1)} %bitcast.4) | data formatting | bytes 2097152
